TPU v7x, 256 devices: a whole 4x4x8 slice. The times are simulated.
256 devices in a mesh: seq: 32 (over z_lo, x, core), cam: 4 (over y), tp: 2 (over z_hi).
Axes of the slice: x: 4, y: 4, z: 8 (z_hi: 2, z_lo: 4; z = z_hi * 4 + z_lo), core: 2. Of those that a mesh axis runs over, the one named last changes fastest.
Arguments:
- pixel_feature: bfloat16 [32768, 2048], P(('seq', 'cam'), 'tp'), may hold values from -6 to 6
- depth_score: float32 [32768, 59], P(('seq', 'cam')), may hold values from 0.05 to 5
- depth_bin: int32 [32768, 4], P(('seq', 'cam')), may hold values from 0 to 58
- cell_owner: int32 [131072, 1], P(('seq', 'cam')), may hold values from 0 to 31; in each aligned block of 1024 rows (0 to 1023, 1024 to 2047, ...) at most 64 rows name the same one
- cell_local: int32 [32768, 4], P(('seq', 'cam')), may hold values from 0 to 7
- frame_keep: int32 [64], replicated, may hold values 0 or 1
- norm_gain: float32 [2048], P('tp'), may hold values from 0.1 to 1.9
- w_query: bfloat16 [2048, 2048], P(None, ('cam', 'tp')), may hold values from -1.5 to 1.5
- w_key: bfloat16 [2048, 2048], P(None, ('cam', 'tp')), may hold values from -0.375 to 0.375
- w_value: bfloat16 [2048, 2048], P(None, ('cam', 'tp')), may hold values from -0.125 to 0.125
Outputs:
- attended: bfloat16 [16384, 2048], P('seq', ('cam', 'tp'))
Inputs may be any that keep to these rules, and one draw needn't show every extreme that they name: `cell_owner`: among the 1024 points of one index of seq and cam (aligned blocks of rows), no owner is named more than 64 times, a bound that some block reaches.
All inputs are finite; a program needn't handle non-finite values.
Results may differ from a plain program's by a relative error of at most 0.028.
The roundings to bfloat16 on the way count: a program that leaves them out, or rounds other values in their place, can miss the bound.
Values may be sent and summed in bfloat16 or wider, within the bound.
A program may use at most 64 MiB of HBM per device.

v0:
```python
import jax
import jax.numpy as jnp
from jax import lax
from jax.sharding import PartitionSpec as P

D = 2048
HD = 128
CELL_DEV = 8
epsilon = 1e-05
block_rows = 512


def attend(state, query, query_start, keys, values, key_start, frame_keep):
    frames = frame_keep.shape[0]
    frame_query = (query_start + jnp.arange(query.shape[0], dtype=jnp.int32)) % frames
    frame_key = (key_start + jnp.arange(keys.shape[0], dtype=jnp.int32)) % frames
    frame_list = jnp.arange(frames, dtype=jnp.int32)
    kept = jnp.sum(
        jnp.where(frame_key[:, None] == frame_list[None, :], frame_keep[None, :], 0), axis=1
    )
    allowed = (frame_key[None, :] <= frame_query[:, None]) & (
        (kept[None, :] > 0) | (frame_key[None, :] == frame_query[:, None])
    )
    scores = jnp.einsum("qhd,khd->hqk", query, keys, preferred_element_type=jnp.float32) * (
        1.0 / HD**0.5
    )
    accum, peak, total = state
    new_peak = jnp.maximum(peak, jnp.max(jnp.where(allowed[None], scores, -1e30), axis=2))
    factor = jnp.exp(peak - new_peak)
    expo = jnp.where(allowed[None], jnp.exp(scores - new_peak[:, :, None]), 0.0)
    mixed = jnp.einsum(
        "hqk,khd->hqd", expo.astype(jnp.bfloat16), values, preferred_element_type=jnp.float32
    )
    return (accum * factor[:, :, None] + mixed, new_peak, total * factor + jnp.sum(expo, axis=2))


def local(
    pixel_feature,
    depth_score,
    depth_bin,
    cell_owner,
    cell_local,
    frame_keep,
    norm_gain,
    w_query,
    w_key,
    w_value,
):
    pixels, half = pixel_feature.shape
    keep_count = depth_bin.shape[1]
    points = pixels * keep_count
    seq_count = lax.axis_size("seq")
    seq_index = lax.axis_index("seq")
    frames = frame_keep.shape[0]
    frames_dev = frames // seq_count
    tokens_dev = CELL_DEV * frames
    capacity = 2 * points // seq_count
    prob = depth_score / jnp.sum(depth_score, axis=1, keepdims=True)
    bins = jnp.arange(depth_score.shape[1], dtype=jnp.int32)
    picked = jnp.sum(
        jnp.where(depth_bin[:, :, None] == bins[None, None, :], prob[:, None, :], 0.0), axis=2
    )
    weight = picked.astype(jnp.bfloat16)
    point_index = jnp.arange(points, dtype=jnp.int32).reshape(pixels, keep_count)
    local_frame = point_index // (points // frames_dev)
    owner = cell_owner[:, 0].reshape(pixels, keep_count)
    owner_flat = owner.reshape(points)
    hits = (owner_flat[:, None] == jnp.arange(seq_count, dtype=jnp.int32)[None, :]).astype(
        jnp.int32
    )
    rank = jnp.sum(jnp.cumsum(hits, axis=0) * hits, axis=1) - 1
    slot = owner_flat * capacity + rank
    point_rows = jnp.repeat(pixel_feature, keep_count, axis=0)
    send_rows = jnp.zeros((seq_count * capacity, half), jnp.bfloat16).at[slot].set(point_rows)
    send_rows = send_rows.reshape(seq_count, capacity, half)
    frame_global = seq_index * frames_dev + local_frame
    describe = jnp.stack(
        [
            weight.reshape(points),
            cell_local.reshape(points).astype(jnp.bfloat16),
            frame_global.reshape(points).astype(jnp.bfloat16),
        ],
        axis=0,
    )
    send_meta = jnp.zeros((3, seq_count * capacity), jnp.bfloat16).at[:, slot].set(describe)
    send_meta = send_meta.reshape(3, seq_count, capacity).transpose(1, 0, 2)
    got_rows, got_meta = (
        lax.all_to_all(send_rows, "seq", split_axis=0, concat_axis=0, tiled=True),
        lax.all_to_all(send_meta, "seq", split_axis=0, concat_axis=0, tiled=True),
    )
    target = (
        got_meta[:, 1, :].astype(jnp.float32) * frames + got_meta[:, 2, :].astype(jnp.float32)
    ).reshape(-1)
    token_ids = jnp.arange(tokens_dev, dtype=jnp.float32)
    mixing = jnp.where(
        token_ids[:, None] == target[None, :], got_meta[:, 0, :].reshape(-1)[None, :], 0
    )
    pooled = jnp.dot(mixing, got_rows.reshape(-1, half), preferred_element_type=jnp.float32)
    bev = lax.psum(pooled, "cam")
    squares = lax.psum(jnp.sum(bev * bev, axis=1), "tp")
    normed = (bev * lax.rsqrt(squares[:, None] / D + epsilon) * norm_gain[None, :]).astype(
        jnp.bfloat16
    )
    width = w_query.shape[1]
    heads_dev = width // HD
    piece = lax.all_gather(normed, "tp", axis=1, tiled=True)
    query_sum = jnp.dot(piece, w_query, preferred_element_type=jnp.float32)
    key_sum = jnp.dot(piece, w_key, preferred_element_type=jnp.float32)
    value_sum = jnp.dot(piece, w_value, preferred_element_type=jnp.float32)
    query = query_sum.astype(jnp.bfloat16).reshape(tokens_dev, heads_dev, HD)
    keys = key_sum.astype(jnp.bfloat16).reshape(tokens_dev, heads_dev, HD)
    values = value_sum.astype(jnp.bfloat16).reshape(tokens_dev, heads_dev, HD)
    query_start = seq_index * tokens_dev
    start_state = (
        jnp.zeros((heads_dev, tokens_dev, HD), jnp.float32),
        jnp.full((heads_dev, tokens_dev), -1e30, jnp.float32),
        jnp.zeros((heads_dev, tokens_dev), jnp.float32),
    )
    piece_keys = lax.all_gather(keys, "seq", axis=0, tiled=True)
    piece_values = lax.all_gather(values, "seq", axis=0, tiled=True)
    count = piece_keys.shape[0]

    def one_block(index, inner):
        block_keys = lax.dynamic_slice_in_dim(piece_keys, index * block_rows, block_rows, 0)
        block_values = lax.dynamic_slice_in_dim(piece_values, index * block_rows, block_rows, 0)
        return attend(
            inner, query, query_start, block_keys, block_values, index * block_rows, frame_keep
        )

    accum, peak, total = lax.fori_loop(0, count // block_rows, one_block, start_state)
    result = accum / total[:, :, None]
    return result.transpose(1, 0, 2).reshape(tokens_dev, width).astype(jnp.bfloat16)


def solution(mesh):
    return jax.shard_map(
        local,
        mesh=mesh,
        in_specs=(
            P(("seq", "cam"), "tp"),
            P(("seq", "cam"), None),
            P(("seq", "cam"), None),
            P(("seq", "cam"), None),
            P(("seq", "cam"), None),
            P(),
            P("tp"),
            P(None, ("cam", "tp")),
            P(None, ("cam", "tp")),
            P(None, ("cam", "tp")),
        ),
        out_specs=P("seq", ("cam", "tp")),
        check_vma=False,
    )
```

profile of v0, /device:TPU:1, one launch (start us, length us, event | category | flops | bytes accessed | tf_op | source)
XLA Modules:
  0.0 587.0 jit_solution(16973022452448787255)
XLA Ops:
  11.1 9.0 %reduce-window.6 = s32[32,8,128]{2,1,0:T(8,128)S(1)} reduce-window(s32[32,8,128]{2,1,0:T(8,128)S(1)} %fusion.34, s32[]{:T(128)} %constant.143.clone.1), window={size=1x1x128 pad=0_0x0_0x127_0}, to_apply=%region_0.0 | reduce-window | flops 4161536 | bytes 262148 | tf_op jit(solution)/shard_map/reduce-window
  22.4 3.3 scatter_custom_fusion
  26.7 10.0 %all-to-all-start = ((bf16[32,3,64]{2,1,0:T(4,128)(2,1)}), bf16[32,3,64]{2,1,0:T(4,128)(2,1)S(1)}, u32[]{:S(2)}, u32[]{:S(2)}) async-start(bf16[32,3,64]{2,1,0:T(4,128)(2,1)} %bitcast.8), calls=%async_computation | async-start | bytes 65536 | tf_op jit(solution)/shard_map/all_to_all | solution.py:89
  36.7 1.7 broadcast_in_dim.171
  38.4 2.1 reshape.333
  40.4 8.6 %scatter_custom_fusion.1 = bf16[2048,1024]{1,0:T(8,128)(2,1)} fusion(s32[1024]{0:T(1024)S(1)} %bitcast.76, bf16[1024,1024]{1,0:T(8,128)(2,1)} %reshape.333, bf16[]{:T(256)} %constant.146.clone.1), kind=kCustom, calls=%fused_computation.44 | custom fusion | bytes 4194816 | tf_op jit(solution)/shard_map/scatter | solution.py:74
  49.0 7.8 %all-to-all-start.1 = ((bf16[32,64,1024]{2,1,0:T(8,128)(2,1)}), bf16[32,64,1024]{2,1,0:T(8,128)(2,1)}, u32[]{:S(2)}, u32[]{:S(2)}) async-start(bf16[32,64,1024]{2,1,0:T(8,128)(2,1)} %bitcast.65), calls=%async_computation.1 | async-start | bytes 8388608 | tf_op jit(solution)/shard_map/all_to_all | solution.py:88
  57.2 92.7 %all-to-all-done.1 = bf16[32,64,1024]{2,1,0:T(8,128)(2,1)} async-done(((bf16[32,64,1024]{2,1,0:T(8,128)(2,1)}), bf16[32,64,1024]{2,1,0:T(8,128)(2,1)}, u32[]{:S(2)}, u32[]{:S(2)}) %all-to-all-start.1) | async-done | bytes 4194336 | tf_op jit(solution)/shard_map/all_to_all | solution.py:88
  149.9 5.9 fusion.22
  155.8 64.2 %all-reduce.2.cloned.1.call-done = f32[512,1024]{1,0:T(8,128)} async-done(((f32[512,1024]{1,0:T(8,128)}), f32[512,1024]{1,0:T(8,128)}) %all-reduce.2.cloned.1.call-update) | async-done | bytes 2097168 | tf_op jit(solution)/shard_map/psum | solution.py:99
  220.0 2.0 multiply_reduce_fusion
  221.9 7.8 %psum.15 = f32[512]{0:T(512)S(1)} all-reduce(f32[512]{0:T(512)S(1)} %multiply_reduce_fusion), channel_id=1, replica_groups=mesh['seq'=32,'cam'=4,'tp'=2] {'tp'}, use_global_device_ids=true, to_apply=%region_9.10 | all-reduce | flops 512 | bytes 4096 | tf_op jit(solution)/shard_map/psum | solution.py:100
  231.2 65.9 %all-gather.4.cloned.1.call-done = bf16[512,2048]{1,0:T(8,128)(2,1)} async-done(((bf16[512,1024]{1,0:T(8,128)(2,1)}), bf16[512,2048]{1,0:T(8,128)(2,1)}) %all-gather.4.cloned.1.call-update) | async-done | bytes 2097168 | tf_op jit(solution)/shard_map/all_gather | solution.py:106
  297.2 2.5 convolution_convert_fusion
  300.6 2.0 convolution_convert_fusion.2
  303.5 2.6 convolution_convert_fusion.1
  306.3 59.7 %all-gather.8.cloned.1.call-done = bf16[16384,2,128]{2,0,1:T(8,128)(2,1)} async-done(((bf16[512,2,128]{2,0,1:T(8,128)(2,1)}), bf16[16384,2,128]{2,0,1:T(8,128)(2,1)}) %all-gather.8.cloned.1.call-update) | async-done | bytes 8388624 | tf_op jit(solution)/shard_map/all_gather | solution.py:120
  366.0 69.0 %all-gather.6.cloned.1.call-done = bf16[16384,2,128]{2,0,1:T(8,128)(2,1)} async-done(((bf16[512,2,128]{2,0,1:T(8,128)(2,1)}), bf16[16384,2,128]{2,0,1:T(8,128)(2,1)}) %all-gather.6.cloned.1.call-update) | async-done | bytes 8388624 | tf_op jit(solution)/shard_map/all_gather | solution.py:119
  435.0 144.5 %while.20 = (s32[]{:T(128)}, f32[2,512,128]{2,1,0:T(8,128)S(1)}, f32[2,512]{1,0:T(2,128)S(1)}, f32[2,512]{1,0:T(2,128)S(1)}, s32[]{:T(128)}, /*index=5*/s32[64]{...) while((s32[]{:T(128)}, f32[2,512,128]{2,1,0:T(8,128)S(1)}, ...), condition=%wide.region_14.15_spmd.clone, body=%wide.region_10.14_spmd.clone.sunk | while | flops 275760128 | bytes 9256399 | solution.py:130
  437.5 2.0 convolution_add_fusion.2
  439.9 1.5 fusion.58
  442.0 2.0 convolution_add_fusion.2
  446.5 2.0 convolution_add_fusion.2
  451.0 2.0 convolution_add_fusion.2
  455.5 2.0 convolution_add_fusion.2
  458.0 1.5 fusion.58
  460.1 2.0 convolution_add_fusion.2
  464.6 2.0 convolution_add_fusion.2
  469.1 2.0 convolution_add_fusion.2
  473.6 2.0 convolution_add_fusion.2
  476.1 1.5 fusion.58
  478.1 2.0 convolution_add_fusion.2
  482.7 2.0 convolution_add_fusion.2
  485.1 1.5 fusion.58
  487.2 2.0 convolution_add_fusion.2
  491.7 2.0 convolution_add_fusion.2
  494.2 1.5 fusion.58
  496.2 2.0 convolution_add_fusion.2
  500.7 2.0 convolution_add_fusion.2
  503.2 1.5 fusion.58
  505.2 2.0 convolution_add_fusion.2
  507.7 1.5 fusion.58
  509.8 2.0 convolution_add_fusion.2
  512.2 1.5 fusion.58
  514.3 2.0 convolution_add_fusion.2
  518.8 2.0 convolution_add_fusion.2
  521.3 1.5 fusion.58
  523.3 2.0 convolution_add_fusion.2
  525.8 1.5 fusion.58
  527.8 2.0 convolution_add_fusion.2
  530.3 1.5 fusion.58
  532.4 2.0 convolution_add_fusion.2
  536.9 2.0 convolution_add_fusion.2
  541.4 2.0 convolution_add_fusion.2
  545.9 2.0 convolution_add_fusion.2
  548.4 1.5 fusion.58
  550.4 2.0 convolution_add_fusion.2
  554.9 2.0 convolution_add_fusion.2
  559.5 2.0 convolution_add_fusion.2
  564.0 2.0 convolution_add_fusion.2
  566.4 1.5 fusion.58
  568.5 2.0 convolution_add_fusion.2
  573.0 2.0 convolution_add_fusion.2
  577.5 2.0 convolution_add_fusion.2
  (331 shorter events, 72.7 us)
Async XLA Ops:
  6.5 290.6 %copy-start = (bf16[2048,256]{1,0:T(8,128)(2,1)S(1)}, bf16[2048,256]{1,0:T(8,128)(2,1)}, u32[]{:S(2)}) copy-start(bf16[2048,256]{1,0:T(8,128)(2,1)} %param.21) | copy-start | bytes 3145732
  26.7 22.4 %all-to-all-start = ((bf16[32,3,64]{2,1,0:T(4,128)(2,1)}), bf16[32,3,64]{2,1,0:T(4,128)(2,1)S(1)}, u32[]{:S(2)}, u32[]{:S(2)}) async-start(bf16[32,3,64]{2,1,0:T(4,128)(2,1)} %bitcast.8), calls=%async_computation | async-start | bytes 65536 | tf_op jit(solution)/shard_map/all_to_all | solution.py:89
  49.0 100.9 %all-to-all-start.1 = ((bf16[32,64,1024]{2,1,0:T(8,128)(2,1)}), bf16[32,64,1024]{2,1,0:T(8,128)(2,1)}, u32[]{:S(2)}, u32[]{:S(2)}) async-start(bf16[32,64,1024]{2,1,0:T(8,128)(2,1)} %bitcast.65), calls=%async_computation.1 | async-start | bytes 8388608 | tf_op jit(solution)/shard_map/all_to_all | solution.py:88
  56.8 163.2 %all-reduce.2.cloned.1.call-start = ((), (), s32[]{:S(2)}) async-start(), calls=%async_computation.2 | async-start | bytes 4194304 | tf_op jit(solution)/shard_map/psum | solution.py:99
  155.7 74.0 %copy-start.3 = (f32[1024]{0:T(1024)S(1)}, f32[1024]{0:T(1024)}, u32[]{:S(2)}) copy-start(f32[1024]{0:T(1024)} %param.18) | copy-start | bytes 12292
  155.8 141.4 %all-gather.4.cloned.1.call-start = ((), (), s32[]{:S(2)}) async-start(), calls=%async_computation.3 | async-start | bytes 3145728 | tf_op jit(solution)/shard_map/all_gather | solution.py:106
  220.0 9.7 %copy-start.1 = (f32[512,1024]{1,0:T(8,128)S(1)}, f32[512,1024]{1,0:T(8,128)}, u32[]{:S(2)}) copy-start(f32[512,1024]{1,0:T(8,128)} %all-reduce.2.cloned.1.call-done) | copy-start | bytes 6291460
  231.0 135.0 %all-gather.8.cloned.1.call-start = ((), (), s32[]{:S(2)}) async-start(), calls=%async_computation.5 | async-start | bytes 8650752 | tf_op jit(solution)/shard_map/all_gather | solution.py:120
  297.2 3.4 copy-start.4
  300.5 134.4 %all-gather.6.cloned.1.call-start = ((), (), s32[]{:S(2)}) async-start(), calls=%async_computation.4 | async-start | bytes 8650752 | tf_op jit(solution)/shard_map/all_gather | solution.py:119
  303.5 131.5 %copy-start.2 = (s32[64]{0:T(128)S(1)}, s32[64]{0:T(128)}, u32[]{:S(2)}) copy-start(s32[64]{0:T(128)} %param.17) | copy-start | bytes 772
Sparse Core Ops, SparseCore 0:
  155.9 64.0 all-reduce.1
  231.1 66.0 all-gather.3
  300.7 65.2 all-gather.7
  367.7 67.1 all-gather.5
where the time goes:
time: 590 us; the launch traced here: 587 us
  waiting for transfers between devices  352 us (60%)
  matrix products  124 us (21%)
  other arithmetic  50.4 us (9%)
  local copies, waits for them, and re-layouts  19.9 us (3%)
  starting transfers between devices  18.1 us (3%)
  between operations  13.3 us (2%)
  blocking collectives  7.76 us (1%)
    all_to_all x1, waiting for transfers between devices, local(): lax.all_to_all(send_rows, 'seq', split_axis=0, concat_axis=0, tiled=True)  92.7 us
    all_gather x1, waiting for transfers between devices, local(): piece_keys = lax.all_gather(keys, 'seq', axis=0, tiled=True)  69 us
    all_gather x1, waiting for transfers between devices, local(): piece = lax.all_gather(normed, 'tp', axis=1, tiled=True)  65.9 us
    psum x1, waiting for transfers between devices, local(): bev = lax.psum(pooled, 'cam')  64.2 us
    dot_general x32, matrix products, attend(): jnp.einsum('hqk,khd->hqd', expo.astype(jnp.bfloat16), values, preferred_e...  62.6 us
    all_gather x1, waiting for transfers between devices, local(): piece_values = lax.all_gather(values, 'seq', axis=0, tiled=True)  59.7 us
    dot_general x32, matrix products, attend(): jnp.einsum('qhd,khd->hqk', query, keys, preferred_element_type=jnp.float32)  48.2 us
    reduce_sum x32, other arithmetic, attend(): jnp.sum(expo, axis=2)  15.9 us
  transfers between devices with their start and end apart: 6, of which 5 were waited for; matrix products, arithmetic and copies ran while one was open for 3% of the time, Pallas kernels for 0%

commit v1 on v0

--- a/solution.py
+++ b/solution.py
@@ -8,6 +8,15 @@
 CELL_DEV = 8
 epsilon = 1e-05
 block_rows = 512
+
+
+def save_leaves_on_mesh(block_here):
+    num_devices = lax.axis_size("cam")
+    w1 = lambda block_next: [(nth, nth ^ block_next) for nth in range(num_devices)]
+    seen_now = block_here
+    for pp in range(num_devices.bit_length() - 1):
+        seen_now = seen_now + lax.ppermute(seen_now, "cam", perm=w1(1 << pp))
+    return seen_now
 
 
 def attend(state, query, query_start, keys, values, key_start, frame_keep):
@@ -96,7 +105,7 @@
         token_ids[:, None] == target[None, :], got_meta[:, 0, :].reshape(-1)[None, :], 0
     )
     pooled = jnp.dot(mixing, got_rows.reshape(-1, half), preferred_element_type=jnp.float32)
-    bev = lax.psum(pooled, "cam")
+    bev = save_leaves_on_mesh(pooled)
     squares = lax.psum(jnp.sum(bev * bev, axis=1), "tp")
     normed = (bev * lax.rsqrt(squares[:, None] / D + epsilon) * norm_gain[None, :]).astype(
         jnp.bfloat16

time: 590 us -> 619 us (1.049)
  waiting for transfers between devices: 352 us -> 379 us
    ppermute x0 -> x2, waiting for transfers between devices: none -> 88.9 us  [save_leaves_on_mesh(): seen_now = seen_now + lax.ppermute(seen_now, 'cam', perm=w1(1 << pp))]
    psum x1 -> x0, waiting for transfers between devices: 64.2 us -> none  [local(): bev = lax.psum(pooled, 'cam')]
  transfers between devices with their start and end apart: 6 -> 7, of which waited for: 5 -> 6; matrix products, arithmetic and copies ran while one was open for 3% -> 3% of each run, Pallas kernels for 0% -> 0%
where the time goes in v1:
time: 619 us; the launch traced here: 616 us
  waiting for transfers between devices  379 us (61%)
  matrix products  123 us (20%)
  other arithmetic  49.3 us (8%)
  starting transfers between devices  22.5 us (4%)
  local copies, waits for them, and re-layouts  19.9 us (3%)
  between operations  13.3 us (2%)
  blocking collectives  7.69 us (1%)
    all_to_all x1, waiting for transfers between devices, local(): lax.all_to_all(send_rows, 'seq', split_axis=0, concat_axis=0, tiled=True)  92.7 us
    ppermute x2, waiting for transfers between devices, save_leaves_on_mesh(): seen_now = seen_now + lax.ppermute(seen_now, 'cam', perm=w1(1 << pp))  88.9 us
    all_gather x1, waiting for transfers between devices, local(): piece_keys = lax.all_gather(keys, 'seq', axis=0, tiled=True)  69.1 us
    all_gather x1, waiting for transfers between devices, local(): piece = lax.all_gather(normed, 'tp', axis=1, tiled=True)  68.4 us
    dot_general x32, matrix products, attend(): jnp.einsum('hqk,khd->hqd', expo.astype(jnp.bfloat16), values, preferred_e...  62.6 us
    all_gather x1, waiting for transfers between devices, local(): piece_values = lax.all_gather(values, 'seq', axis=0, tiled=True)  59.7 us
    dot_general x32, matrix products, attend(): jnp.einsum('qhd,khd->hqk', query, keys, preferred_element_type=jnp.float32)  48.3 us
    reduce_sum x32, other arithmetic, attend(): jnp.sum(expo, axis=2)  15.9 us
  transfers between devices with their start and end apart: 7, of which 6 were waited for; matrix products, arithmetic and copies ran while one was open for 3% of the time, Pallas kernels for 0%

profile of v1, /device:TPU:1, one launch (start us, length us, event | category | flops | bytes accessed | tf_op | source)
XLA Modules:
  0.0 616.1 jit_solution(2584130061162451371)
XLA Ops:
  11.1 9.0 %reduce-window.6 = s32[32,8,128]{2,1,0:T(8,128)S(1)} reduce-window(s32[32,8,128]{2,1,0:T(8,128)S(1)} %fusion.34, s32[]{:T(128)} %constant.143.clone.1), window={size=1x1x128 pad=0_0x0_0x127_0}, to_apply=%region_0.0 | reduce-window | flops 4161536 | bytes 262148 | tf_op jit(solution)/shard_map/reduce-window
  22.4 3.3 scatter_custom_fusion
  26.7 10.0 %all-to-all-start = ((bf16[32,3,64]{2,1,0:T(4,128)(2,1)}), bf16[32,3,64]{2,1,0:T(4,128)(2,1)S(1)}, u32[]{:S(2)}, u32[]{:S(2)}) async-start(bf16[32,3,64]{2,1,0:T(4,128)(2,1)} %bitcast.8), calls=%async_computation | async-start | bytes 65536 | tf_op jit(solution)/shard_map/all_to_all | solution.py:98
  36.7 1.7 broadcast_in_dim.171
  38.4 2.1 reshape.333
  40.4 8.6 %scatter_custom_fusion.1 = bf16[2048,1024]{1,0:T(8,128)(2,1)} fusion(s32[1024]{0:T(1024)S(1)} %bitcast.76, bf16[1024,1024]{1,0:T(8,128)(2,1)} %reshape.333, bf16[]{:T(256)} %constant.146.clone.1), kind=kCustom, calls=%fused_computation.44 | custom fusion | bytes 4194816 | tf_op jit(solution)/shard_map/scatter | solution.py:83
  49.0 7.8 %all-to-all-start.1 = ((bf16[32,64,1024]{2,1,0:T(8,128)(2,1)}), bf16[32,64,1024]{2,1,0:T(8,128)(2,1)}, u32[]{:S(2)}, u32[]{:S(2)}) async-start(bf16[32,64,1024]{2,1,0:T(8,128)(2,1)} %bitcast.65), calls=%async_computation.1 | async-start | bytes 8388608 | tf_op jit(solution)/shard_map/all_to_all | solution.py:97
  57.1 92.7 %all-to-all-done.1 = bf16[32,64,1024]{2,1,0:T(8,128)(2,1)} async-done(((bf16[32,64,1024]{2,1,0:T(8,128)(2,1)}), bf16[32,64,1024]{2,1,0:T(8,128)(2,1)}, u32[]{:S(2)}, u32[]{:S(2)}) %all-to-all-start.1) | async-done | bytes 4194336 | tf_op jit(solution)/shard_map/all_to_all | solution.py:97
  149.8 4.5 fusion.22
  154.4 1.6 collective-permute-start
  155.9 44.9 %collective-permute-done = f32[512,1024]{1,0:T(8,128)S(1)} collective-permute-done((f32[512,1024]{1,0:T(8,128)S(1)}, f32[512,1024]{1,0:T(8,128)S(1)}, u32[]{:S(2)}, u32[]{:S(2)}) %collective-permute-start) | collective-permute-done | bytes 2097184 | tf_op jit(solution)/shard_map/ppermute | solution.py:18
  201.4 3.0 collective-permute-start.1
  204.4 44.0 %collective-permute-done.1 = f32[512,1024]{1,0:T(8,128)S(1)} collective-permute-done((f32[512,1024]{1,0:T(8,128)S(1)}, f32[512,1024]{1,0:T(8,128)S(1)}, u32[]{:S(2)}, u32[]{:S(2)}) %collective-permute-start.1) | collective-permute-done | bytes 2097184 | tf_op jit(solution)/shard_map/ppermute | solution.py:18
  248.7 7.7 %psum.7 = f32[512]{0:T(512)S(1)} all-reduce(f32[512]{0:T(512)S(1)} %get-tuple-element.315), channel_id=1, replica_groups=mesh['seq'=32,'cam'=4,'tp'=2] {'tp'}, use_global_device_ids=true, to_apply=%region_8.9 | all-reduce | flops 512 | bytes 4096 | tf_op jit(solution)/shard_map/psum | solution.py:109
  257.7 68.4 %all-gather.4.cloned.1.call-done = bf16[512,2048]{1,0:T(8,128)(2,1)} async-done(((bf16[512,1024]{1,0:T(8,128)(2,1)}), bf16[512,2048]{1,0:T(8,128)(2,1)}) %all-gather.4.cloned.1.call-update) | async-done | bytes 2097168 | tf_op jit(solution)/shard_map/all_gather | solution.py:115
  326.1 2.5 convolution_convert_fusion
  329.5 2.0 convolution_convert_fusion.2
  332.4 2.6 convolution_convert_fusion.1
  335.2 59.7 %all-gather.8.cloned.1.call-done = bf16[16384,2,128]{2,0,1:T(8,128)(2,1)} async-done(((bf16[512,2,128]{2,0,1:T(8,128)(2,1)}), bf16[16384,2,128]{2,0,1:T(8,128)(2,1)}) %all-gather.8.cloned.1.call-update) | async-done | bytes 8388624 | tf_op jit(solution)/shard_map/all_gather | solution.py:129
  394.9 69.1 %all-gather.6.cloned.1.call-done = bf16[16384,2,128]{2,0,1:T(8,128)(2,1)} async-done(((bf16[512,2,128]{2,0,1:T(8,128)(2,1)}), bf16[16384,2,128]{2,0,1:T(8,128)(2,1)}) %all-gather.6.cloned.1.call-update) | async-done | bytes 8388624 | tf_op jit(solution)/shard_map/all_gather | solution.py:128
  464.0 144.7 %while.20 = (s32[]{:T(128)}, f32[2,512,128]{2,1,0:T(8,128)S(1)}, f32[2,512]{1,0:T(2,128)S(1)}, f32[2,512]{1,0:T(2,128)S(1)}, s32[]{:T(128)}, /*index=5*/s32[64]{...) while((s32[]{:T(128)}, f32[2,512,128]{2,1,0:T(8,128)S(1)}, ...), condition=%wide.region_13.14_spmd.clone, body=%wide.region_9.13_spmd.clone.sunk | while | flops 275760128 | bytes 9256399 | solution.py:139
  466.5 2.0 convolution_add_fusion.2
  469.0 1.5 fusion.58
  471.1 2.0 convolution_add_fusion.2
  473.5 1.5 fusion.58
  475.6 2.0 convolution_add_fusion.2
  478.1 1.5 fusion.58
  480.1 2.0 convolution_add_fusion.2
  482.6 1.5 fusion.58
  484.6 2.0 convolution_add_fusion.2
  487.1 1.5 fusion.58
  489.1 2.0 convolution_add_fusion.2
  491.6 1.5 fusion.58
  493.7 2.0 convolution_add_fusion.2
  496.1 1.5 fusion.58
  498.2 2.0 convolution_add_fusion.2
  500.7 1.5 fusion.58
  502.7 2.0 convolution_add_fusion.2
  505.2 1.5 fusion.58
  507.2 2.0 convolution_add_fusion.2
  509.7 1.5 fusion.58
  511.8 2.0 convolution_add_fusion.2
  514.2 1.5 fusion.58
  516.3 2.0 convolution_add_fusion.2
  520.8 2.0 convolution_add_fusion.2
  525.3 2.0 convolution_add_fusion.2
  529.8 2.0 convolution_add_fusion.2
  534.4 2.0 convolution_add_fusion.2
  538.9 2.0 convolution_add_fusion.2
  543.4 2.0 convolution_add_fusion.2
  547.9 2.0 convolution_add_fusion.2
  552.5 2.0 convolution_add_fusion.2
  557.0 2.0 convolution_add_fusion.2
  561.5 2.0 convolution_add_fusion.2
  566.0 2.0 convolution_add_fusion.2
  570.5 2.0 convolution_add_fusion.2
  575.1 2.0 convolution_add_fusion.2
  579.6 2.0 convolution_add_fusion.2
  584.1 2.0 convolution_add_fusion.2
  588.6 2.0 convolution_add_fusion.2
  593.2 2.0 convolution_add_fusion.2
  597.7 2.0 convolution_add_fusion.2
  602.2 2.0 convolution_add_fusion.2
  606.7 2.0 convolution_add_fusion.2
  (331 shorter events, 76.4 us)
Async XLA Ops:
  6.5 319.5 %copy-start = (bf16[2048,256]{1,0:T(8,128)(2,1)S(1)}, bf16[2048,256]{1,0:T(8,128)(2,1)}, u32[]{:S(2)}) copy-start(bf16[2048,256]{1,0:T(8,128)(2,1)} %param.21) | copy-start | bytes 3145732
  26.7 22.3 %all-to-all-start = ((bf16[32,3,64]{2,1,0:T(4,128)(2,1)}), bf16[32,3,64]{2,1,0:T(4,128)(2,1)S(1)}, u32[]{:S(2)}, u32[]{:S(2)}) async-start(bf16[32,3,64]{2,1,0:T(4,128)(2,1)} %bitcast.8), calls=%async_computation | async-start | bytes 65536 | tf_op jit(solution)/shard_map/all_to_all | solution.py:98
  49.0 100.9 %all-to-all-start.1 = ((bf16[32,64,1024]{2,1,0:T(8,128)(2,1)}), bf16[32,64,1024]{2,1,0:T(8,128)(2,1)}, u32[]{:S(2)}, u32[]{:S(2)}) async-start(bf16[32,64,1024]{2,1,0:T(8,128)(2,1)} %bitcast.65), calls=%async_computation.1 | async-start | bytes 8388608 | tf_op jit(solution)/shard_map/all_to_all | solution.py:97
  56.8 269.3 %all-gather.4.cloned.1.call-start = ((), (), s32[]{:S(2)}) async-start(), calls=%async_computation.2 | async-start | bytes 3145728 | tf_op jit(solution)/shard_map/all_gather | solution.py:115
  154.4 46.5 %collective-permute-start = (f32[512,1024]{1,0:T(8,128)S(1)}, f32[512,1024]{1,0:T(8,128)S(1)}, u32[]{:S(2)}, u32[]{:S(2)}) collective-permute-start(f32[512,1024]{1,0:T(8,128)S(1)} %fusion.22), channel_id=1, source_target_pairs={{0,2},{2,0},{4,6},{6,4},{1,3},{3,1},{5,7},{7,5},{8,10},{10,8},{12,... | collective-permute-start | bytes 6291464 | tf_op jit(solution)/shard_map/ppermute | solution.py:18
  201.4 55.0 %copy-start.2 = (f32[1024]{0:T(1024)S(1)}, f32[1024]{0:T(1024)}, u32[]{:S(2)}) copy-start(f32[1024]{0:T(1024)} %param.18) | copy-start | bytes 12292
  201.4 47.0 %collective-permute-start.1 = (f32[512,1024]{1,0:T(8,128)S(1)}, f32[512,1024]{1,0:T(8,128)S(1)}, u32[]{:S(2)}, u32[]{:S(2)}) collective-permute-start(f32[512,1024]{1,0:T(8,128)S(1)} %add.221), channel_id=1, source_target_pairs={{0,4},{2,6},{4,0},{6,2},{1,5},{3,7},{5,1},{7,3},{8,12},{10,14},{12... | collective-permute-start | bytes 6291464 | tf_op jit(solution)/shard_map/ppermute | solution.py:18
  257.6 137.3 %all-gather.8.cloned.1.call-start = ((), (), s32[]{:S(2)}) async-start(), calls=%async_computation.4 | async-start | bytes 8650752 | tf_op jit(solution)/shard_map/all_gather | solution.py:129
  326.1 3.4 copy-start.3
  329.4 134.6 %all-gather.6.cloned.1.call-start = ((), (), s32[]{:S(2)}) async-start(), calls=%async_computation.3 | async-start | bytes 8650752 | tf_op jit(solution)/shard_map/all_gather | solution.py:128
  332.4 131.6 %copy-start.1 = (s32[64]{0:T(128)S(1)}, s32[64]{0:T(128)}, u32[]{:S(2)}) copy-start(s32[64]{0:T(128)} %param.17) | copy-start | bytes 772
Sparse Core Ops, SparseCore 0:
  257.8 68.2 all-gather.3
  329.6 65.2 all-gather.7
  396.8 67.1 all-gather.5
